TPU v7x, 128 devices: a whole 4x4x4 slice. The times are simulated.
128 devices in a mesh: face: 4 (over y), sub: 32 (over x, z, core).
Axes of the slice: x: 4, y: 4, z: 4, core: 2. Of those that a mesh axis runs over, the one named last changes fastest.
Arguments:
- field: bfloat16 [3, 4, 128, 128, 256], P(None, 'face', 'sub'), may hold values from -6 to 6
- dw_kernel: float32 [9, 256], replicated, may hold values from -2 to 2
- dw_bias: float32 [256], replicated, may hold values from -3 to 3
- zonal_kernel: float32 [7, 256], replicated, may hold values from -2 to 2
- zonal_bias: float32 [256], replicated, may hold values from -3 to 3
- norm_gain: float32 [256], replicated, may hold values from 0.1 to 1.9
- w_in: bfloat16 [256, 768], replicated, may hold values from -0.375 to 0.375
- w_out: bfloat16 [768, 256], replicated, may hold values from -0.21875 to 0.21875
- layer_scale: float32 [256], replicated, may hold values from 0.5 to 1.5
Outputs:
- output: bfloat16 [3, 4, 128, 128, 256], P(None, 'face', 'sub')
All inputs are finite; a program needn't handle non-finite values.
Results may differ from a plain program's by a relative error of at most 0.001.
The roundings to bfloat16 on the way count: a program that leaves them out, or rounds other values in their place, can miss the bound.
Values may be sent and summed in bfloat16 or wider, within the bound.
A program may use at most 64 MiB of HBM per device.

v0:
```python
import jax
import jax.numpy as jnp
from jax import lax
from jax.sharding import PartitionSpec as P

TAPS = 7
DILATION = 4


def extended_2(block, sides, width, periodic):
    for axis, dim in sides:
        count = lax.axis_size(axis)
        forward = [(i, i + 1) for i in range(count - 1)]
        if periodic:
            forward.append((count - 1, 0))
        backward = [(target, source) for source, target in forward]
        low = lax.ppermute(
            lax.slice_in_dim(block, block.shape[dim] - width, None, axis=dim), axis, forward
        )
        high = lax.ppermute(lax.slice_in_dim(block, 0, width, axis=dim), axis, backward)
        block = jnp.concatenate([low, block, high], axis=dim)
    return block


def cut_along(value, dim, size):
    before, after = (value.shape[:dim], value.shape[dim + 1 :])
    return jnp.moveaxis(value.reshape(*before, size, -1, *after), dim, 0)


def sum_at_owner(value, axis, dim):
    parts = cut_along(value, dim, lax.axis_size(axis))
    arrived = lax.all_to_all(parts, axis, split_axis=0, concat_axis=0, tiled=True)
    return arrived.astype(jnp.float32).sum(axis=0)


def joined_along(parts, dim):
    dims = list(parts.shape[1:])
    dims[dim] *= parts.shape[0]
    return jnp.moveaxis(parts, 0, dim).reshape(dims)


def copy_for_each(value, axis):
    size = lax.axis_size(axis)
    return lax.all_to_all(
        jnp.broadcast_to(value[None], (size, *value.shape)), axis, 0, 0, tiled=True
    )


def gathered_copies(value, axis, dim):
    return joined_along(copy_for_each(value, axis), dim)


def cycle_place(facet, column, row_pos, side):
    cycle = (facet + 2) * side - column - row_pos - 1
    along = jnp.where(
        facet == 0,
        column + cycle - side,
        jnp.where((facet == 1) & (cycle < 2 * side), column + cycle - 2 * side, column),
    )
    arc_len = jnp.minimum(jnp.minimum(cycle, side), 4 * side - cycle)
    return (cycle, along, arc_len)


def cycle_cell(cycle, along, side):
    north = (cycle < 2 * side) & (along >= cycle - side)
    middle = jnp.logical_not(north) & (along < 3 * side - cycle)
    facet = jnp.where(north, jnp.int32(0), jnp.where(middle, jnp.int32(1), jnp.int32(2)))
    column = jnp.where(
        north,
        along - cycle + side,
        jnp.where(middle & (cycle < 2 * side), along + 2 * side - cycle, along),
    )
    row_pos = (facet + 2) * side - 1 - cycle - column
    return (facet, column, row_pos)


def take_row(segment_block, permutation):
    return jnp.take(segment_block, permutation, axis=2)


def reorder(values, order):
    return jax.vmap(take_row, in_axes=(1, 0), out_axes=1)(values, order)


def shards(
    field, dw_kernel, dw_bias, zonal_kernel, zonal_bias, norm_gain, w_in, w_out, layer_scale
):
    local_field = field[:, 0]
    rows_here = local_field.shape[1]
    side_cells = local_field.shape[2]
    channels = local_field.shape[3]
    edge_index = side_cells - 1
    sub_count = lax.axis_size("sub")
    quad_total = lax.axis_size("face")
    sub_index = lax.axis_index("sub")
    quad_index = lax.axis_index("face")
    row_start = sub_index * rows_here
    side_pair = jnp.stack([local_field[1, :, 0], local_field[2, :, edge_index]])
    beside_all = extended_2(side_pair, (("face", 0),), 1, True)
    last_lines = jnp.where(
        sub_index == sub_count - 1, local_field[:, rows_here - 1], jnp.zeros_like(local_field[:, 0])
    )
    first_lines = jnp.where(sub_index == 0, local_field[:, 0], jnp.zeros_like(local_field[:, 0]))
    rim_lines = jnp.swapaxes(jnp.concatenate([last_lines, first_lines], 0), 0, 1)
    pieces = sum_at_owner(rim_lines.astype(jnp.float32).astype(jnp.bfloat16), "sub", 0).astype(
        jnp.bfloat16
    )
    strips = jnp.stack(
        [
            pieces[:, 0],
            pieces[:, 1],
            local_field[2, :, 0],
            pieces[:, 5],
            local_field[0, :, edge_index],
            pieces[:, 3],
        ]
    )
    near = extended_2(strips, (("face", 0),), 3, True)
    wanted = jnp.stack([near[10], pieces[:, 2], near[11], near[1], near[2], pieces[:, 4]])
    lines = gathered_copies(wanted, "sub", 1)
    left_slice = near[0]
    right_slice = near[9]
    face_top = lines[0:3]
    face_bottom = lines[3:6]
    left_side = jnp.stack([local_field[1, :, edge_index], beside_all[0], left_slice])
    right_side = jnp.stack([right_slice, local_field[0, :, 0], beside_all[3]])
    widened = jnp.concatenate([left_side[:, :, None], local_field, right_side[:, :, None]], 2)
    extended = extended_2(widened, (("sub", 1),), 1, False)
    corner = jnp.zeros((3, 1, channels), local_field.dtype)
    face_top = jnp.concatenate([corner, face_top, corner], 1)
    face_bottom = jnp.concatenate([corner, face_bottom, corner], 1)
    first_row = jnp.where(sub_index == 0, face_top, extended[:, 0])
    final_row = jnp.where(sub_index == sub_count - 1, face_bottom, extended[:, rows_here + 1])
    padded = jnp.concatenate(
        [first_row[:, None], extended[:, 1 : rows_here + 1], final_row[:, None]], 1
    )
    total = jnp.zeros((3, rows_here, side_cells, channels), jnp.float32) + dw_bias
    for i in range(3):
        for j in range(3):
            total = total + dw_kernel[3 * i + j] * padded[
                :, i : i + rows_here, j : j + side_cells
            ].astype(jnp.float32)
    mixed = total.astype(jnp.bfloat16)
    shard_count = quad_total * sub_count
    shard_id = quad_index * sub_count + sub_index
    blocks = side_cells // shard_count
    row_ids = row_start + lax.broadcasted_iota(jnp.int32, (rows_here, shard_count), 0)
    shard_ids = lax.broadcasted_iota(jnp.int32, (rows_here, shard_count), 1)
    order = (-row_ids - 1 - shard_ids) % shard_count
    sending = reorder(mixed.reshape(3, rows_here, blocks, shard_count, channels), order)
    arrived = lax.all_to_all(sending, ("face", "sub"), split_axis=3, concat_axis=3, tiled=True)
    buffer = arrived.reshape(3, rows_here, blocks, quad_total, sub_count, channels)
    shape_out = (3, rows_here, blocks, quad_total, sub_count)
    facet = lax.broadcasted_iota(jnp.int32, shape_out, 0)
    row_local = lax.broadcasted_iota(jnp.int32, shape_out, 1)
    block_ids = lax.broadcasted_iota(jnp.int32, shape_out, 2)
    quad_out = lax.broadcasted_iota(jnp.int32, shape_out, 3)
    sub_source = lax.broadcasted_iota(jnp.int32, shape_out, 4)
    row_pos = sub_source * rows_here + row_local
    residue = (-row_pos - 1 - shard_id) % shard_count
    column = shard_count * block_ids + residue
    cycle, along, arc_len = cycle_place(facet, column, row_pos, side_cells)
    place = quad_out * arc_len + along
    flat = buffer.reshape(-1, channels)
    half = TAPS // 2
    accum = jnp.zeros(shape_out + (channels,), jnp.float32) + zonal_bias
    for k in range(TAPS):
        moved = (place + DILATION * (k - half)) % (4 * arc_len)
        quad_new = moved // arc_len
        along_new = moved % arc_len
        facet_new, column_new, row_new = cycle_cell(cycle, along_new, side_cells)
        index = (
            ((facet_new * rows_here + row_new % rows_here) * blocks + column_new // shard_count)
            * quad_total
            + quad_new
        ) * sub_count + row_new // rows_here
        gathered = jnp.take(flat, index.reshape(-1), axis=0).reshape(shape_out + (channels,))
        accum = accum + zonal_kernel[k] * gathered.astype(jnp.float32)
    zonal = accum.astype(jnp.bfloat16)
    returned = lax.all_to_all(
        zonal.reshape(3, rows_here, blocks, shard_count, channels),
        ("face", "sub"),
        split_axis=3,
        concat_axis=3,
        tiled=True,
    )
    restored = reorder(returned, order).reshape(3, rows_here, side_cells, channels)

    def finish(pair):
        zonal_face, input_face = pair
        values = zonal_face.reshape(-1, channels).astype(jnp.float32)
        mean = jnp.mean(values, -1, keepdims=True)
        spread = jnp.mean(jnp.square(values - mean), -1, keepdims=True)
        normed = ((values - mean) * lax.rsqrt(spread + 1e-06) * norm_gain).astype(jnp.bfloat16)
        hidden = jax.nn.gelu(
            jnp.dot(normed, w_in, preferred_element_type=jnp.float32), approximate=False
        ).astype(jnp.bfloat16)
        branch = jnp.dot(hidden, w_out, preferred_element_type=jnp.float32)
        source = input_face.reshape(-1, channels).astype(jnp.float32)
        result = (source + layer_scale * branch).astype(jnp.bfloat16)
        return result.reshape(rows_here, side_cells, channels)

    output = lax.map(finish, (restored, local_field))
    return output[:, None]


def solution(mesh):
    in_specs = (P(None, "face", "sub", None, None), P(), P(), P(), P(), P(), P(), P(), P())
    out_specs = P(None, "face", "sub", None, None)
    return jax.shard_map(shards, mesh=mesh, in_specs=in_specs, out_specs=out_specs, check_vma=False)
```

profile of v0, /device:TPU:1, one launch (start us, length us, event | category | flops | bytes accessed | tf_op | source)
XLA Modules:
  0.0 164.4 jit_solution(5760792183229900761)
XLA Ops:
  0.0 1.1 fusion.90
  1.2 0.9 copy.316
  2.1 9.4 %all-to-all-start = ((bf16[32,4,6,256]{3,1,2,0:T(4,128)(2,1)}), bf16[32,4,6,256]{3,1,2,0:T(4,128)(2,1)S(1)}, u32[]{:S(2)}, u32[]{:S(2)}) async-start(bf16[32,4,6,256]{3,1,2,0:T(4,128)(2,1)} %copy.316), calls=%async_computation | async-start | bytes 786432 | tf_op jit(solution)/shard_map/all_to_all | solution.py:32
  11.6 2.8 %collective-permute-start.3 = (bf16[1,4,256]{2,1,0:T(4,128)(2,1)S(1)}, bf16[1,4,256]{2,1,0:T(4,128)(2,1)S(1)}, u32[]{:S(2)}, u32[]{:S(2)}) collective-permute-start(bf16[1,4,256]{2,1,0:T(4,128)(2,1)S(1)} %bitcast.200), channel_id=1, source_target_pairs={{32,0},{64,32},{96,64},{0,96},{33,1},{65,33},{97,65},{1,97},{34,2}... | collective-permute-start | bytes 6152 | tf_op jit(solution)/shard_map/ppermute | solution.py:20
  15.4 0.4 compare_and_fusion.6
  15.7 6.1 %all-to-all-done = bf16[32,4,6,256]{3,1,2,0:T(4,128)(2,1)S(1)} async-done(((bf16[32,4,6,256]{3,1,2,0:T(4,128)(2,1)}), bf16[32,4,6,256]{3,1,2,0:T(4,128)(2,1)S(1)}, u32[]{:S(2)}, u32[]{:S(2)}) %all-to-all-start) | async-done | bytes 393248 | tf_op jit(solution)/shard_map/all_to_all | solution.py:32
  22.0 2.8 %collective-permute-start = (bf16[3,4,256]{2,1,0:T(4,128)(2,1)S(1)}, bf16[3,4,256]{2,1,0:T(4,128)(2,1)S(1)}, u32[]{:S(2)}, u32[]{:S(2)}) collective-permute-start(bf16[3,4,256]{2,1,0:T(4,128)(2,1)S(1)} %pad_maximum_fusion.10), channel_id=1, source_target_pairs={{32,0},{64,32},{96,64},{0,96},{33,1},{65,33},{97,65},{1,97},{34,2}... | collective-permute-start | bytes 18440 | tf_op jit(solution)/shard_map/ppermute | solution.py:20
  24.9 0.7 collective-permute-done
  25.6 3.0 %collective-permute-done.1 = bf16[3,4,256]{2,1,0:T(4,128)(2,1)S(1)} collective-permute-done((bf16[3,4,256]{2,1,0:T(4,128)(2,1)S(1)}, bf16[3,4,256]{2,1,0:T(4,128)(2,1)S(1)}, u32[]{:S(2)}, u32[]{:S(2)}) %collective-permute-start.1) | collective-permute-done | bytes 6176 | tf_op jit(solution)/shard_map/ppermute | solution.py:17
  28.6 0.9 broadcast_in_dim.92
  29.5 5.0 %all-to-all-start.1 = ((bf16[32,6,4,256]{3,2,1,0:T(4,128)(2,1)}), bf16[32,6,4,256]{3,2,1,0:T(4,128)(2,1)S(1)}, u32[]{:S(2)}, u32[]{:S(2)}) async-start(bf16[32,6,4,256]{3,2,1,0:T(4,128)(2,1)} %broadcast_in_dim.92), calls=%async_computation.1 | async-start | bytes 786432 | tf_op jit(solution)/shard_map/all_to_all | solution.py:44
  34.8 3.5 %collective-permute-start.4 = (bf16[3,1,130,256]{3,2,1,0:T(8,128)(2,1)S(1)}, bf16[3,1,130,256]{3,2,1,0:T(8,128)(2,1)S(1)}, u32[]{:S(2)}, u32[]{:S(2)}) collective-permute-start(bf16[3,1,130,256]{3,2,1,0:T(8,128)(2,1)S(1)} %get-tuple-element.174), channel_id=1, source_target_pairs={{0,1},{1,2},{2,3},{3,4},{4,5},{5,6},{6,7},{7,8},{8,9},{9,10},{10,1... | collective-permute-start | bytes 599048 | tf_op jit(solution)/shard_map/ppermute | solution.py:17
  38.4 1.9 %collective-permute-start.5 = (bf16[3,1,130,256]{3,2,1,0:T(8,128)(2,1)S(1)}, bf16[3,1,130,256]{3,2,1,0:T(8,128)(2,1)S(1)}, u32[]{:S(2)}, u32[]{:S(2)}) collective-permute-start(bf16[3,1,130,256]{3,2,1,0:T(8,128)(2,1)S(1)} %get-tuple-element.175), channel_id=1, source_target_pairs={{1,0},{2,1},{3,2},{4,3},{5,4},{6,5},{7,6},{8,7},{9,8},{10,9},{11,1... | collective-permute-start | bytes 599048 | tf_op jit(solution)/shard_map/ppermute | solution.py:20
  40.3 4.5 %all-to-all-done.1 = bf16[32,6,4,256]{3,2,1,0:T(4,128)(2,1)S(1)} async-done(((bf16[32,6,4,256]{3,2,1,0:T(4,128)(2,1)}), bf16[32,6,4,256]{3,2,1,0:T(4,128)(2,1)S(1)}, u32[]{:S(2)}, u32[]{:S(2)}) %all-to-all-start.1) | async-done | bytes 393248 | tf_op jit(solution)/shard_map/all_to_all | solution.py:44
  45.2 0.4 collective-permute-done.5
  45.8 0.4 maximum_maximum_fusion
  46.5 2.2 %fusion.86 = bf16[4,3,128,256]{3,2,0,1:T(8,128)(2,1)S(1)} fusion(bf16[3,5,130,256]{3,2,1,0:T(8,128)(2,1)S(1)} %get-tuple-element.173, f32[256]{0:T(256)S(1)} %bitcast.197, f32[256]{0:T(256)S(1)} %bitcast.198, f32[256]{0:T(256)S(1)} %bitcast.191, bf16[3,4,1,256]{3,2,1,0:T(2,128)(2,1)S(1)} %copy.320, bf16[3,4,128,256]{3,2,1,0:T(8,128)(2,1)S(1)} %bitcast.164, ...), kind=kLoop, calls=%fused_computation.134 | loop fusion | flops 13369344 | bytes 6313984 | tf_op jit(solution)/shard_map/vmap(jit(_take))/transpose | solution.py:78
  48.7 0.7 copy.325
  49.4 2.8 %gather_fusion = bf16[512,3,256]{2,1,0:T(4,128)(2,1)S(1)} fusion(bf16[4,3,128,256]{3,1,2,0:T(4,128)(2,1)S(1)} %copy.325, s32[512]{0:T(512)S(1)} %fusion.195), kind=kCustom, calls=%fused_computation.clone | custom fusion | bytes 1576960 | tf_op jit(solution)/shard_map/vmap(jit(_take))/gather | solution.py:78
  52.2 1.7 %fusion.85 = bf16[3,4,1,128,256]{4,1,2,0,3:T(4,128)(2,1)} fusion(bf16[4,128,3,256]{3,2,1,0:T(4,128)(2,1)S(1)} %bitcast.168, pred[4,128]{0,1:T(8,128)(4,1)S(1)} %copy.315), kind=kLoop, calls=%fused_computation.126 | loop fusion | flops 393216 | bytes 1573376 | tf_op jit(solution)/shard_map/vmap()/transpose | solution.py:82
  53.9 7.8 %all-to-all-start.2 = ((bf16[3,4,1,128,256]{4,1,2,0,3:T(4,128)(2,1)}), bf16[3,4,1,128,256]{4,1,2,0,3:T(4,128)(2,1)S(1)}, u32[]{:S(2)}, u32[]{:S(2)}) async-start(bf16[3,4,1,128,256]{4,1,2,0,3:T(4,128)(2,1)} %fusion.85), calls=%async_computation.2 | async-start | bytes 1572864 | tf_op jit(solution)/shard_map/all_to_all | solution.py:151
  61.8 1.6 compare_and_fusion.5
  63.5 14.5 %all-to-all-done.2 = bf16[3,4,1,128,256]{4,1,2,0,3:T(4,128)(2,1)S(1)} async-done(((bf16[3,4,1,128,256]{4,1,2,0,3:T(4,128)(2,1)}), bf16[3,4,1,128,256]{4,1,2,0,3:T(4,128)(2,1)S(1)}, u32[]{:S(2)}, u32[]{:S(2)}) %all-to-all-start.2) | async-done | bytes 786464 | tf_op jit(solution)/shard_map/all_to_all | solution.py:151
  78.1 5.4 %gather_fusion.2 = bf16[1536,256]{1,0:T(8,128)(2,1)} fusion(bf16[1536,256]{1,0:T(8,128)(2,1)S(1)} %bitcast.153, s32[2048]{0:T(1024)S(1)} %get-tuple-element.227), kind=kCustom, calls=%fused_computation.3.clone | custom fusion | bytes 1579008 | tf_op jit(solution)/shard_map/jit(_take)/gather | solution.py:177
  83.5 5.3 %gather_fusion.3 = bf16[1536,256]{1,0:T(8,128)(2,1)} fusion(bf16[1536,256]{1,0:T(8,128)(2,1)S(1)} %bitcast.154, s32[2048]{0:T(1024)S(1)} %get-tuple-element.226), kind=kCustom, calls=%fused_computation.4.clone | custom fusion | bytes 1579008 | tf_op jit(solution)/shard_map/jit(_take)/gather | solution.py:177
  88.8 5.4 %gather_fusion.4 = bf16[1536,256]{1,0:T(8,128)(2,1)} fusion(bf16[1536,256]{1,0:T(8,128)(2,1)S(1)} %bitcast.155, s32[2048]{0:T(1024)S(1)} %get-tuple-element.225), kind=kCustom, calls=%fused_computation.5.clone | custom fusion | bytes 1579008 | tf_op jit(solution)/shard_map/jit(_take)/gather | solution.py:177
  94.2 5.3 %gather_fusion.5 = bf16[1536,256]{1,0:T(8,128)(2,1)} fusion(bf16[1536,256]{1,0:T(8,128)(2,1)S(1)} %bitcast.156, s32[2048]{0:T(1024)S(1)} %get-tuple-element.224), kind=kCustom, calls=%fused_computation.6.clone | custom fusion | bytes 1579008 | tf_op jit(solution)/shard_map/jit(_take)/gather | solution.py:177
  99.5 5.4 %gather_fusion.6 = bf16[1536,256]{1,0:T(8,128)(2,1)} fusion(bf16[1536,256]{1,0:T(8,128)(2,1)S(1)} %bitcast.157, s32[2048]{0:T(1024)S(1)} %get-tuple-element.223), kind=kCustom, calls=%fused_computation.7.clone | custom fusion | bytes 1579008 | tf_op jit(solution)/shard_map/jit(_take)/gather | solution.py:177
  104.9 4.8 %gather_fusion.1 = bf16[1536,256]{1,0:T(8,128)(2,1)S(1)} fusion(bf16[1536,256]{1,0:T(8,128)(2,1)S(1)} %bitcast.158, s32[2048]{0:T(1024)S(1)} %pad_clamp_fusion.6), kind=kCustom, calls=%fused_computation.1.clone | custom fusion | bytes 1579008 | tf_op jit(solution)/shard_map/jit(_take)/gather | solution.py:177
  109.7 4.8 %gather_fusion.7 = bf16[1536,256]{1,0:T(8,128)(2,1)S(1)} fusion(bf16[1536,256]{1,0:T(8,128)(2,1)S(1)} %bitcast.159, s32[2048]{0:T(1024)S(1)} %get-tuple-element.222), kind=kCustom, calls=%fused_computation.8.clone | custom fusion | bytes 1579008 | tf_op jit(solution)/shard_map/jit(_take)/gather | solution.py:177
  114.4 1.5 broadcast_select_fusion.5
  116.2 0.8 copy-done.2
  117.7 0.8 copy-done.1
  119.3 0.4 copy-done.9
  119.7 1.1 fusion.77
  120.9 1.5 copy.328
  122.4 4.7 %all-to-all-start.3 = ((bf16[3,4,1,128,256]{4,1,2,0,3:T(4,128)(2,1)}), bf16[3,4,1,128,256]{4,1,2,0,3:T(4,128)(2,1)S(1)}, u32[]{:S(2)}, u32[]{:S(2)}) async-start(bf16[3,4,1,128,256]{4,1,2,0,3:T(4,128)(2,1)} %copy.328), calls=%async_computation.3 | async-start | bytes 1572864 | tf_op jit(solution)/shard_map/all_to_all | solution.py:180
  127.1 16.4 %all-to-all-done.3 = bf16[3,4,1,128,256]{4,1,2,0,3:T(4,128)(2,1)S(1)} async-done(((bf16[3,4,1,128,256]{4,1,2,0,3:T(4,128)(2,1)}), bf16[3,4,1,128,256]{4,1,2,0,3:T(4,128)(2,1)S(1)}, u32[]{:S(2)}, u32[]{:S(2)}) %all-to-all-start.3) | async-done | bytes 786464 | tf_op jit(solution)/shard_map/all_to_all | solution.py:180
  143.5 0.4 copy.346
  143.9 2.8 %gather_fusion.8 = bf16[512,3,256]{2,1,0:T(4,128)(2,1)S(1)} fusion(bf16[4,3,128,256]{3,1,2,0:T(4,128)(2,1)S(1)} %bitcast.169, s32[512]{0:T(512)S(1)} %fusion.195), kind=kCustom, calls=%fused_computation.2.clone | custom fusion | bytes 1576960 | tf_op jit(solution)/shard_map/vmap(jit(_take))/gather | solution.py:78
  146.9 0.5 copy-done.5
  147.4 17.1 %while.10 = (s32[]{:T(128)}, bf16[3,4,128,256]{3,2,1,0:T(8,128)(2,1)}, bf16[3,4,128,256]{3,2,1,0:T(8,128)(2,1)S(1)}, f32[256]{0:T(256)S(1)}, bf16[3,4,128,256]{3...) while((s32[]{:T(128)}, ...), condition=%wide.region_4.7_spmd, body=%wide.region_1.6_spmd.sunk | while | flops 430178816 | bytes 6838949 | solution.py:203
  148.5 3.8 %fusion.214 = bf16[512,256]{1,0:T(8,128)(2,1)S(1)} fusion(bf16[768,256]{1,0:T(8,128)(2,1)S(1)} %copy-done.11, bf16[512,256]{1,0:T(8,128)(2,1)S(1)} %fusion.213, bf16[256,768]{1,0:T(8,128)(2,1)S(1)} %copy-done.10, bf16[512,256]{1,0:T(8,128)(2,1)S(1)} %bitcast.167, f32[256]{0:T(256)S(1)} %get-tuple-element.302), kind=kOutput, calls=%fused_computation.30.clone.1 | convolution fusion | flops 428736512 | bytes 1573888 | tf_op jit(solution)/shard_map/while/body/eval_jaxpr/dot_general | solution.py:198
  152.3 0.7 constant_dynamic-update-slice_fusion.7
  154.2 3.8 %fusion.214 = bf16[512,256]{1,0:T(8,128)(2,1)S(1)} fusion(bf16[768,256]{1,0:T(8,128)(2,1)S(1)} %copy-done.11, bf16[512,256]{1,0:T(8,128)(2,1)S(1)} %fusion.213, bf16[256,768]{1,0:T(8,128)(2,1)S(1)} %copy-done.10, bf16[512,256]{1,0:T(8,128)(2,1)S(1)} %bitcast.167, f32[256]{0:T(256)S(1)} %get-tuple-element.302), kind=kOutput, calls=%fused_computation.30.clone.1 | convolution fusion | flops 428736512 | bytes 1573888 | tf_op jit(solution)/shard_map/while/body/eval_jaxpr/dot_general | solution.py:198
  158.0 0.7 constant_dynamic-update-slice_fusion.7
  159.9 3.8 %fusion.214 = bf16[512,256]{1,0:T(8,128)(2,1)S(1)} fusion(bf16[768,256]{1,0:T(8,128)(2,1)S(1)} %copy-done.11, bf16[512,256]{1,0:T(8,128)(2,1)S(1)} %fusion.213, bf16[256,768]{1,0:T(8,128)(2,1)S(1)} %copy-done.10, bf16[512,256]{1,0:T(8,128)(2,1)S(1)} %bitcast.167, f32[256]{0:T(256)S(1)} %get-tuple-element.302), kind=kOutput, calls=%fused_computation.30.clone.1 | convolution fusion | flops 428736512 | bytes 1573888 | tf_op jit(solution)/shard_map/while/body/eval_jaxpr/dot_general | solution.py:198
  163.7 0.7 constant_dynamic-update-slice_fusion.7
  (116 shorter events, 7.8 us)
Async XLA Ops:
  1.1 10.4 %copy-start = (bf16[3,1,4,128,256]{4,3,2,1,0:T(8,128)(2,1)S(1)}, bf16[3,1,4,128,256]{4,3,2,1,0:T(8,128)(2,1)}, u32[]{:S(2)}) copy-start(bf16[3,1,4,128,256]{4,3,2,1,0:T(8,128)(2,1)} %param.15) | copy-start | bytes 2359300
  1.1 13.4 %copy-start.7 = (f32[9,256]{1,0:T(8,128)S(1)}, f32[9,256]{1,0:T(8,128)}, u32[]{:S(2)}) copy-start(f32[9,256]{1,0:T(8,128)} %param.16) | copy-start | bytes 27652
  2.1 19.7 %all-to-all-start = ((bf16[32,4,6,256]{3,1,2,0:T(4,128)(2,1)}), bf16[32,4,6,256]{3,1,2,0:T(4,128)(2,1)S(1)}, u32[]{:S(2)}, u32[]{:S(2)}) async-start(bf16[32,4,6,256]{3,1,2,0:T(4,128)(2,1)} %copy.316), calls=%async_computation | async-start | bytes 786432 | tf_op jit(solution)/shard_map/all_to_all | solution.py:32
  11.6 23.0 %collective-permute-start.3 = (bf16[1,4,256]{2,1,0:T(4,128)(2,1)S(1)}, bf16[1,4,256]{2,1,0:T(4,128)(2,1)S(1)}, u32[]{:S(2)}, u32[]{:S(2)}) collective-permute-start(bf16[1,4,256]{2,1,0:T(4,128)(2,1)S(1)} %bitcast.200), channel_id=1, source_target_pairs={{32,0},{64,32},{96,64},{0,96},{33,1},{65,33},{97,65},{1,97},{34,2}... | collective-permute-start | bytes 6152 | tf_op jit(solution)/shard_map/ppermute | solution.py:20
  14.4 20.3 %collective-permute-start.2 = (bf16[1,4,256]{2,1,0:T(4,128)(2,1)S(1)}, bf16[1,4,256]{2,1,0:T(4,128)(2,1)S(1)}, u32[]{:S(2)}, u32[]{:S(2)}) collective-permute-start(bf16[1,4,256]{2,1,0:T(4,128)(2,1)S(1)} %bitcast.199), channel_id=1, source_target_pairs={{0,32},{32,64},{64,96},{96,0},{1,33},{33,65},{65,97},{97,1},{2,34}... | collective-permute-start | bytes 6152 | tf_op jit(solution)/shard_map/ppermute | solution.py:17
  22.0 3.6 %collective-permute-start = (bf16[3,4,256]{2,1,0:T(4,128)(2,1)S(1)}, bf16[3,4,256]{2,1,0:T(4,128)(2,1)S(1)}, u32[]{:S(2)}, u32[]{:S(2)}) collective-permute-start(bf16[3,4,256]{2,1,0:T(4,128)(2,1)S(1)} %pad_maximum_fusion.10), channel_id=1, source_target_pairs={{32,0},{64,32},{96,64},{0,96},{33,1},{65,33},{97,65},{1,97},{34,2}... | collective-permute-start | bytes 18440 | tf_op jit(solution)/shard_map/ppermute | solution.py:20
  24.8 3.8 %collective-permute-start.1 = (bf16[3,4,256]{2,1,0:T(4,128)(2,1)S(1)}, bf16[3,4,256]{2,1,0:T(4,128)(2,1)S(1)}, u32[]{:S(2)}, u32[]{:S(2)}) collective-permute-start(bf16[3,4,256]{2,1,0:T(4,128)(2,1)S(1)} %pad_maximum_fusion.11), channel_id=1, source_target_pairs={{0,32},{32,64},{64,96},{96,0},{1,33},{33,65},{65,97},{97,1},{2,34}... | collective-permute-start | bytes 18440 | tf_op jit(solution)/shard_map/ppermute | solution.py:17
  29.5 15.3 %all-to-all-start.1 = ((bf16[32,6,4,256]{3,2,1,0:T(4,128)(2,1)}), bf16[32,6,4,256]{3,2,1,0:T(4,128)(2,1)S(1)}, u32[]{:S(2)}, u32[]{:S(2)}) async-start(bf16[32,6,4,256]{3,2,1,0:T(4,128)(2,1)} %broadcast_in_dim.92), calls=%async_computation.1 | async-start | bytes 786432 | tf_op jit(solution)/shard_map/all_to_all | solution.py:44
  34.8 10.3 %collective-permute-start.4 = (bf16[3,1,130,256]{3,2,1,0:T(8,128)(2,1)S(1)}, bf16[3,1,130,256]{3,2,1,0:T(8,128)(2,1)S(1)}, u32[]{:S(2)}, u32[]{:S(2)}) collective-permute-start(bf16[3,1,130,256]{3,2,1,0:T(8,128)(2,1)S(1)} %get-tuple-element.174), channel_id=1, source_target_pairs={{0,1},{1,2},{2,3},{3,4},{4,5},{5,6},{6,7},{7,8},{8,9},{9,10},{10,1... | collective-permute-start | bytes 599048 | tf_op jit(solution)/shard_map/ppermute | solution.py:17
  38.4 7.2 %collective-permute-start.5 = (bf16[3,1,130,256]{3,2,1,0:T(8,128)(2,1)S(1)}, bf16[3,1,130,256]{3,2,1,0:T(8,128)(2,1)S(1)}, u32[]{:S(2)}, u32[]{:S(2)}) collective-permute-start(bf16[3,1,130,256]{3,2,1,0:T(8,128)(2,1)S(1)} %get-tuple-element.175), channel_id=1, source_target_pairs={{1,0},{2,1},{3,2},{4,3},{5,4},{6,5},{7,6},{8,7},{9,8},{10,9},{11,1... | collective-permute-start | bytes 599048 | tf_op jit(solution)/shard_map/ppermute | solution.py:20
  45.8 0.7 copy-start.8
  53.9 9.5 %copy-start.6 = (f32[7,256]{1,0:T(8,128)S(1)}, f32[7,256]{1,0:T(8,128)}, u32[]{:S(2)}) copy-start(f32[7,256]{1,0:T(8,128)} %param.18) | copy-start | bytes 21508
  53.9 24.1 %all-to-all-start.2 = ((bf16[3,4,1,128,256]{4,1,2,0,3:T(4,128)(2,1)}), bf16[3,4,1,128,256]{4,1,2,0,3:T(4,128)(2,1)S(1)}, u32[]{:S(2)}, u32[]{:S(2)}) async-start(bf16[3,4,1,128,256]{4,1,2,0,3:T(4,128)(2,1)} %fusion.85), calls=%async_computation.2 | async-start | bytes 1572864 | tf_op jit(solution)/shard_map/all_to_all | solution.py:151
  114.4 1.5 copy-start.4
  115.9 1.1 copy-start.2
  116.2 1.2 copy-start.3
  117.3 1.2 copy-start.1
  119.0 0.7 copy-start.9
  122.4 21.1 %all-to-all-start.3 = ((bf16[3,4,1,128,256]{4,1,2,0,3:T(4,128)(2,1)}), bf16[3,4,1,128,256]{4,1,2,0,3:T(4,128)(2,1)S(1)}, u32[]{:S(2)}, u32[]{:S(2)}) async-start(bf16[3,4,1,128,256]{4,1,2,0,3:T(4,128)(2,1)} %copy.328), calls=%async_computation.3 | async-start | bytes 1572864 | tf_op jit(solution)/shard_map/all_to_all | solution.py:180
  146.7 0.7 copy-start.5
  146.7 0.7 copy-start.12
  147.4 1.0 copy-start.10
  147.4 1.1 copy-start.11
  153.1 1.0 copy-start.10
  153.1 1.1 copy-start.11
  158.8 1.0 copy-start.10
  158.8 1.1 copy-start.11
where the time goes:
time: 165 us; the launch traced here: 164 us
  local copies, waits for them, and re-layouts  54.2 us (33%)
  waiting for transfers between devices  45.5 us (28%)
  starting transfers between devices  38.1 us (23%)
  other arithmetic  14.4 us (9%)
  matrix products  11.5 us (7%)
    gather x7, local copies, waits for them, and re-layouts, shards(): jnp.take(flat, index.reshape(-1), axis=0).reshape(shape_out + (channels,))  36.3 us
    all_to_all x1, waiting for transfers between devices, shards(): lax.all_to_all(zonal.reshape(3, rows_here, blocks, shard_count, channels)...  16.4 us
    all_to_all x1, waiting for transfers between devices, shards(): lax.all_to_all(sending, ('face', 'sub'), split_axis=3, concat_axis=3, til...  14.5 us
    dot_general x3, matrix products, finish(): branch = jnp.dot(hidden, w_out, preferred_element_type=jnp.float32)  11.5 us
    all_to_all x1, starting transfers between devices, sum_at_owner(): lax.all_to_all(parts, axis, split_axis=0, concat_axis=0, tiled=True)  9.42 us
    all_to_all x1, starting transfers between devices, shards(): lax.all_to_all(sending, ('face', 'sub'), split_axis=3, concat_axis=3, til...  7.84 us
    ppermute x3, starting transfers between devices, extended_2(): lax.ppermute(lax.slice_in_dim(block, 0, width, axis=dim), axis, backward)  7.53 us
    all_to_all x1, waiting for transfers between devices, sum_at_owner(): lax.all_to_all(parts, axis, split_axis=0, concat_axis=0, tiled=True)  6.07 us
  transfers between devices with their start and end apart: 10, of which 7 were waited for; matrix products, arithmetic and copies ran while one was open for 3% of the time, Pallas kernels for 0%

commit v1 on v0

--- a/solution.py
+++ b/solution.py
@@ -148,7 +148,9 @@
     shard_ids = lax.broadcasted_iota(jnp.int32, (rows_here, shard_count), 1)
     order = (-row_ids - 1 - shard_ids) % shard_count
     sending = reorder(mixed.reshape(3, rows_here, blocks, shard_count, channels), order)
-    arrived = lax.all_to_all(sending, ("face", "sub"), split_axis=3, concat_axis=3, tiled=True)
+    cells = jnp.split(sending, lax.axis_size(("face", "sub")), axis=3)
+    arrived_2 = lax.all_to_all(jnp.stack(cells), ("face", "sub"), 0, 0)
+    arrived = jnp.concatenate(arrived_2, axis=3)
     buffer = arrived.reshape(3, rows_here, blocks, quad_total, sub_count, channels)
     shape_out = (3, rows_here, blocks, quad_total, sub_count)
     facet = lax.broadcasted_iota(jnp.int32, shape_out, 0)

time: 165 us -> 241 us (1.46)
  local copies, waits for them, and re-layouts: 54.2 us -> 131 us
    unnamed x31 -> x158, local copies, waits for them, and re-layouts: 2.99 us -> 78.8 us
  transfers between devices with their start and end apart: 10 -> 10, of which waited for: 7 -> 7; matrix products, arithmetic and copies ran while one was open for 3% -> 2% of each run, Pallas kernels for 0% -> 0%
where the time goes in v1:
time: 241 us; the launch traced here: 240 us
  local copies, waits for them, and re-layouts  131 us (54%)
  waiting for transfers between devices  45.5 us (19%)
  starting transfers between devices  38.1 us (16%)
  other arithmetic  13.5 us (6%)
  matrix products  11.5 us (5%)
    unnamed x158, local copies, waits for them, and re-layouts  78.8 us
    gather x7, local copies, waits for them, and re-layouts, shards(): jnp.take(flat, index.reshape(-1), axis=0).reshape(shape_out + (channels,))  36.3 us
    all_to_all x1, waiting for transfers between devices, shards(): lax.all_to_all(zonal.reshape(3, rows_here, blocks, shard_count, channels)...  16.4 us
    all_to_all x1, waiting for transfers between devices, shards(): arrived_2 = lax.all_to_all(jnp.stack(cells), ('face', 'sub'), 0, 0)  14.5 us
    dot_general x3, matrix products, finish(): branch = jnp.dot(hidden, w_out, preferred_element_type=jnp.float32)  11.5 us
    all_to_all x1, starting transfers between devices, sum_at_owner(): lax.all_to_all(parts, axis, split_axis=0, concat_axis=0, tiled=True)  9.42 us
    all_to_all x1, starting transfers between devices, shards(): arrived_2 = lax.all_to_all(jnp.stack(cells), ('face', 'sub'), 0, 0)  7.84 us
    ppermute x3, starting transfers between devices, extended_2(): lax.ppermute(lax.slice_in_dim(block, 0, width, axis=dim), axis, backward)  7.53 us
  transfers between devices with their start and end apart: 10, of which 7 were waited for; matrix products, arithmetic and copies ran while one was open for 2% of the time, Pallas kernels for 0%

profile of v1, /device:TPU:1, one launch (start us, length us, event | category | flops | bytes accessed | tf_op | source)
XLA Modules:
  0.0 240.0 jit_solution(4553650336770166513)
XLA Ops:
  0.0 1.1 fusion.90
  1.2 0.9 copy.433
  2.1 9.4 %all-to-all-start = ((bf16[32,4,6,256]{3,1,2,0:T(4,128)(2,1)}), bf16[32,4,6,256]{3,1,2,0:T(4,128)(2,1)S(1)}, u32[]{:S(2)}, u32[]{:S(2)}) async-start(bf16[32,4,6,256]{3,1,2,0:T(4,128)(2,1)} %copy.433), calls=%async_computation | async-start | bytes 786432 | tf_op jit(solution)/shard_map/all_to_all | solution.py:32
  11.6 2.8 %collective-permute-start.3 = (bf16[1,4,256]{2,1,0:T(4,128)(2,1)S(1)}, bf16[1,4,256]{2,1,0:T(4,128)(2,1)S(1)}, u32[]{:S(2)}, u32[]{:S(2)}) collective-permute-start(bf16[1,4,256]{2,1,0:T(4,128)(2,1)S(1)} %bitcast.714), channel_id=1, source_target_pairs={{32,0},{64,32},{96,64},{0,96},{33,1},{65,33},{97,65},{1,97},{34,2}... | collective-permute-start | bytes 6152 | tf_op jit(solution)/shard_map/ppermute | solution.py:20
  15.7 6.1 %all-to-all-done = bf16[32,4,6,256]{3,1,2,0:T(4,128)(2,1)S(1)} async-done(((bf16[32,4,6,256]{3,1,2,0:T(4,128)(2,1)}), bf16[32,4,6,256]{3,1,2,0:T(4,128)(2,1)S(1)}, u32[]{:S(2)}, u32[]{:S(2)}) %all-to-all-start) | async-done | bytes 393248 | tf_op jit(solution)/shard_map/all_to_all | solution.py:32
  22.0 2.8 %collective-permute-start = (bf16[3,4,256]{2,1,0:T(4,128)(2,1)S(1)}, bf16[3,4,256]{2,1,0:T(4,128)(2,1)S(1)}, u32[]{:S(2)}, u32[]{:S(2)}) collective-permute-start(bf16[3,4,256]{2,1,0:T(4,128)(2,1)S(1)} %pad_maximum_fusion.10), channel_id=1, source_target_pairs={{32,0},{64,32},{96,64},{0,96},{33,1},{65,33},{97,65},{1,97},{34,2}... | collective-permute-start | bytes 18440 | tf_op jit(solution)/shard_map/ppermute | solution.py:20
  24.9 0.7 collective-permute-done
  25.6 3.0 %collective-permute-done.1 = bf16[3,4,256]{2,1,0:T(4,128)(2,1)S(1)} collective-permute-done((bf16[3,4,256]{2,1,0:T(4,128)(2,1)S(1)}, bf16[3,4,256]{2,1,0:T(4,128)(2,1)S(1)}, u32[]{:S(2)}, u32[]{:S(2)}) %collective-permute-start.1) | collective-permute-done | bytes 6176 | tf_op jit(solution)/shard_map/ppermute | solution.py:17
  28.6 0.9 broadcast_in_dim.92
  29.5 5.0 %all-to-all-start.1 = ((bf16[32,6,4,256]{3,2,1,0:T(4,128)(2,1)}), bf16[32,6,4,256]{3,2,1,0:T(4,128)(2,1)S(1)}, u32[]{:S(2)}, u32[]{:S(2)}) async-start(bf16[32,6,4,256]{3,2,1,0:T(4,128)(2,1)} %broadcast_in_dim.92), calls=%async_computation.1 | async-start | bytes 786432 | tf_op jit(solution)/shard_map/all_to_all | solution.py:44
  34.8 3.5 %collective-permute-start.4 = (bf16[3,1,130,256]{3,2,1,0:T(8,128)(2,1)S(1)}, bf16[3,1,130,256]{3,2,1,0:T(8,128)(2,1)S(1)}, u32[]{:S(2)}, u32[]{:S(2)}) collective-permute-start(bf16[3,1,130,256]{3,2,1,0:T(8,128)(2,1)S(1)} %get-tuple-element.166), channel_id=1, source_target_pairs={{0,1},{1,2},{2,3},{3,4},{4,5},{5,6},{6,7},{7,8},{8,9},{9,10},{10,1... | collective-permute-start | bytes 599048 | tf_op jit(solution)/shard_map/ppermute | solution.py:17
  38.4 1.9 collective-permute-start.5
  40.3 4.5 %all-to-all-done.1 = bf16[32,6,4,256]{3,2,1,0:T(4,128)(2,1)S(1)} async-done(((bf16[32,6,4,256]{3,2,1,0:T(4,128)(2,1)}), bf16[32,6,4,256]{3,2,1,0:T(4,128)(2,1)S(1)}, u32[]{:S(2)}, u32[]{:S(2)}) %all-to-all-start.1) | async-done | bytes 393248 | tf_op jit(solution)/shard_map/all_to_all | solution.py:44
  46.5 2.2 fusion.86
  48.7 0.7 copy.442
  49.4 2.8 %gather_fusion = bf16[512,3,256]{2,1,0:T(4,128)(2,1)S(1)} fusion(bf16[4,3,128,256]{3,1,2,0:T(4,128)(2,1)S(1)} %copy.442, s32[512]{0:T(512)S(1)} %fusion.195), kind=kCustom, calls=%fused_computation.clone | custom fusion | bytes 1576960 | tf_op jit(solution)/shard_map/vmap(jit(_take))/gather | solution.py:78
  52.1 0.9 fusion.85
  53.0 0.6 constant_dynamic-update-slice_fusion.133
  54.8 0.6 constant_dynamic-update-slice_fusion.130
  62.0 0.6 constant_dynamic-update-slice_fusion.118
  66.2 0.6 constant_dynamic-update-slice_fusion.111
  73.3 0.6 constant_dynamic-update-slice_fusion.99
  77.5 0.6 constant_dynamic-update-slice_fusion.92
  129.5 7.8 %all-to-all-start.2 = ((bf16[128,3,4,1,1,256]{5,2,1,4,3,0:T(4,128)(2,1)}), bf16[128,3,4,1,1,256]{5,2,1,4,3,0:T(4,128)(2,1)S(1)}, u32[]{:S(2)}, u32[]{:S(2)}) async-start(bf16[128,3,4,1,1,256]{5,2,1,4,3,0:T(4,128)(2,1)} %constant_dynamic-update-slice_fusion.6), calls=%async_computation.2 | async-start | bytes 1572864 | tf_op jit(solution)/shard_map/all_to_all | solution.py:152
  137.3 1.6 compare_and_fusion.5
  139.0 14.5 %all-to-all-done.2 = bf16[128,3,4,1,1,256]{5,2,1,4,3,0:T(4,128)(2,1)S(1)} async-done(((bf16[128,3,4,1,1,256]{5,2,1,4,3,0:T(4,128)(2,1)}), bf16[128,3,4,1,1,256]{5,2,1,4,3,0:T(4,128)(2,1)S(1)}, u32[]{:S(2)}, u32[]{:S(2)}) %all-to-all-start.2) | async-done | bytes 786464 | tf_op jit(solution)/shard_map/all_to_all | solution.py:152
  153.7 5.4 %gather_fusion.2 = bf16[1536,256]{1,0:T(8,128)(2,1)} fusion(bf16[1536,256]{1,0:T(8,128)(2,1)S(1)} %bitcast.666, s32[2048]{0:T(1024)S(1)} %get-tuple-element.219), kind=kCustom, calls=%fused_computation.3.clone | custom fusion | bytes 1579008 | tf_op jit(solution)/shard_map/jit(_take)/gather | solution.py:179
  159.0 5.3 %gather_fusion.3 = bf16[1536,256]{1,0:T(8,128)(2,1)} fusion(bf16[1536,256]{1,0:T(8,128)(2,1)S(1)} %bitcast.667, s32[2048]{0:T(1024)S(1)} %get-tuple-element.218), kind=kCustom, calls=%fused_computation.4.clone | custom fusion | bytes 1579008 | tf_op jit(solution)/shard_map/jit(_take)/gather | solution.py:179
  164.4 5.4 %gather_fusion.4 = bf16[1536,256]{1,0:T(8,128)(2,1)} fusion(bf16[1536,256]{1,0:T(8,128)(2,1)S(1)} %bitcast.668, s32[2048]{0:T(1024)S(1)} %get-tuple-element.217), kind=kCustom, calls=%fused_computation.5.clone | custom fusion | bytes 1579008 | tf_op jit(solution)/shard_map/jit(_take)/gather | solution.py:179
  169.7 5.3 %gather_fusion.5 = bf16[1536,256]{1,0:T(8,128)(2,1)} fusion(bf16[1536,256]{1,0:T(8,128)(2,1)S(1)} %bitcast.669, s32[2048]{0:T(1024)S(1)} %get-tuple-element.216), kind=kCustom, calls=%fused_computation.6.clone | custom fusion | bytes 1579008 | tf_op jit(solution)/shard_map/jit(_take)/gather | solution.py:179
  175.1 5.4 %gather_fusion.6 = bf16[1536,256]{1,0:T(8,128)(2,1)} fusion(bf16[1536,256]{1,0:T(8,128)(2,1)S(1)} %bitcast.670, s32[2048]{0:T(1024)S(1)} %get-tuple-element.215), kind=kCustom, calls=%fused_computation.7.clone | custom fusion | bytes 1579008 | tf_op jit(solution)/shard_map/jit(_take)/gather | solution.py:179
  180.4 4.8 %gather_fusion.1 = bf16[1536,256]{1,0:T(8,128)(2,1)S(1)} fusion(bf16[1536,256]{1,0:T(8,128)(2,1)S(1)} %bitcast.671, s32[2048]{0:T(1024)S(1)} %pad_clamp_fusion.6), kind=kCustom, calls=%fused_computation.1.clone | custom fusion | bytes 1579008 | tf_op jit(solution)/shard_map/jit(_take)/gather | solution.py:179
  185.2 4.8 %gather_fusion.7 = bf16[1536,256]{1,0:T(8,128)(2,1)S(1)} fusion(bf16[1536,256]{1,0:T(8,128)(2,1)S(1)} %bitcast.672, s32[2048]{0:T(1024)S(1)} %get-tuple-element.214), kind=kCustom, calls=%fused_computation.8.clone | custom fusion | bytes 1579008 | tf_op jit(solution)/shard_map/jit(_take)/gather | solution.py:179
  190.0 1.5 broadcast_select_fusion.5
  191.8 0.8 copy-done.2
  193.2 0.8 copy-done.1
  195.3 1.2 fusion.77
  196.4 1.5 copy.445
  197.9 4.7 %all-to-all-start.3 = ((bf16[3,4,1,128,256]{4,1,2,0,3:T(4,128)(2,1)}), bf16[3,4,1,128,256]{4,1,2,0,3:T(4,128)(2,1)S(1)}, u32[]{:S(2)}, u32[]{:S(2)}) async-start(bf16[3,4,1,128,256]{4,1,2,0,3:T(4,128)(2,1)} %copy.445), calls=%async_computation.3 | async-start | bytes 1572864 | tf_op jit(solution)/shard_map/all_to_all | solution.py:182
  202.7 16.4 %all-to-all-done.3 = bf16[3,4,1,128,256]{4,1,2,0,3:T(4,128)(2,1)S(1)} async-done(((bf16[3,4,1,128,256]{4,1,2,0,3:T(4,128)(2,1)}), bf16[3,4,1,128,256]{4,1,2,0,3:T(4,128)(2,1)S(1)}, u32[]{:S(2)}, u32[]{:S(2)}) %all-to-all-start.3) | async-done | bytes 786464 | tf_op jit(solution)/shard_map/all_to_all | solution.py:182
  219.4 2.8 %gather_fusion.8 = bf16[512,3,256]{2,1,0:T(4,128)(2,1)S(1)} fusion(bf16[4,3,128,256]{3,1,2,0:T(4,128)(2,1)S(1)} %bitcast.682, s32[512]{0:T(512)S(1)} %fusion.195), kind=kCustom, calls=%fused_computation.2.clone | custom fusion | bytes 1576960 | tf_op jit(solution)/shard_map/vmap(jit(_take))/gather | solution.py:78
  222.9 17.1 %while.10 = (s32[]{:T(128)}, bf16[3,4,128,256]{3,2,1,0:T(8,128)(2,1)}, bf16[3,4,128,256]{3,2,1,0:T(8,128)(2,1)S(1)}, f32[256]{0:T(256)S(1)}, bf16[3,4,128,256]{3...) while((s32[]{:T(128)}, ...), condition=%wide.region_4.7_spmd, body=%wide.region_1.6_spmd.sunk | while | flops 430178816 | bytes 6838949 | solution.py:205
  224.1 3.8 %fusion.214 = bf16[512,256]{1,0:T(8,128)(2,1)S(1)} fusion(bf16[768,256]{1,0:T(8,128)(2,1)S(1)} %copy-done.11, bf16[512,256]{1,0:T(8,128)(2,1)S(1)} %fusion.213, bf16[256,768]{1,0:T(8,128)(2,1)S(1)} %copy-done.10, bf16[512,256]{1,0:T(8,128)(2,1)S(1)} %bitcast.680, f32[256]{0:T(256)S(1)} %get-tuple-element.294), kind=kOutput, calls=%fused_computation.30.clone.1 | convolution fusion | flops 428736512 | bytes 1573888 | tf_op jit(solution)/shard_map/while/body/eval_jaxpr/dot_general | solution.py:200
  227.9 0.7 constant_dynamic-update-slice_fusion.135
  229.7 3.8 %fusion.214 = bf16[512,256]{1,0:T(8,128)(2,1)S(1)} fusion(bf16[768,256]{1,0:T(8,128)(2,1)S(1)} %copy-done.11, bf16[512,256]{1,0:T(8,128)(2,1)S(1)} %fusion.213, bf16[256,768]{1,0:T(8,128)(2,1)S(1)} %copy-done.10, bf16[512,256]{1,0:T(8,128)(2,1)S(1)} %bitcast.680, f32[256]{0:T(256)S(1)} %get-tuple-element.294), kind=kOutput, calls=%fused_computation.30.clone.1 | convolution fusion | flops 428736512 | bytes 1573888 | tf_op jit(solution)/shard_map/while/body/eval_jaxpr/dot_general | solution.py:200
  233.6 0.7 constant_dynamic-update-slice_fusion.135
  235.4 3.8 %fusion.214 = bf16[512,256]{1,0:T(8,128)(2,1)S(1)} fusion(bf16[768,256]{1,0:T(8,128)(2,1)S(1)} %copy-done.11, bf16[512,256]{1,0:T(8,128)(2,1)S(1)} %fusion.213, bf16[256,768]{1,0:T(8,128)(2,1)S(1)} %copy-done.10, bf16[512,256]{1,0:T(8,128)(2,1)S(1)} %bitcast.680, f32[256]{0:T(256)S(1)} %get-tuple-element.294), kind=kOutput, calls=%fused_computation.30.clone.1 | convolution fusion | flops 428736512 | bytes 1573888 | tf_op jit(solution)/shard_map/while/body/eval_jaxpr/dot_general | solution.py:200
  239.3 0.7 constant_dynamic-update-slice_fusion.135
  (244 shorter events, 83.1 us)
Async XLA Ops:
  1.1 10.4 %copy-start = (bf16[3,1,4,128,256]{4,3,2,1,0:T(8,128)(2,1)S(1)}, bf16[3,1,4,128,256]{4,3,2,1,0:T(8,128)(2,1)}, u32[]{:S(2)}) copy-start(bf16[3,1,4,128,256]{4,3,2,1,0:T(8,128)(2,1)} %param.15) | copy-start | bytes 2359300
  1.1 13.4 %copy-start.7 = (f32[9,256]{1,0:T(8,128)S(1)}, f32[9,256]{1,0:T(8,128)}, u32[]{:S(2)}) copy-start(f32[9,256]{1,0:T(8,128)} %param.16) | copy-start | bytes 27652
  2.1 19.7 %all-to-all-start = ((bf16[32,4,6,256]{3,1,2,0:T(4,128)(2,1)}), bf16[32,4,6,256]{3,1,2,0:T(4,128)(2,1)S(1)}, u32[]{:S(2)}, u32[]{:S(2)}) async-start(bf16[32,4,6,256]{3,1,2,0:T(4,128)(2,1)} %copy.433), calls=%async_computation | async-start | bytes 786432 | tf_op jit(solution)/shard_map/all_to_all | solution.py:32
  11.6 23.0 %collective-permute-start.3 = (bf16[1,4,256]{2,1,0:T(4,128)(2,1)S(1)}, bf16[1,4,256]{2,1,0:T(4,128)(2,1)S(1)}, u32[]{:S(2)}, u32[]{:S(2)}) collective-permute-start(bf16[1,4,256]{2,1,0:T(4,128)(2,1)S(1)} %bitcast.714), channel_id=1, source_target_pairs={{32,0},{64,32},{96,64},{0,96},{33,1},{65,33},{97,65},{1,97},{34,2}... | collective-permute-start | bytes 6152 | tf_op jit(solution)/shard_map/ppermute | solution.py:20
  14.4 20.3 %collective-permute-start.2 = (bf16[1,4,256]{2,1,0:T(4,128)(2,1)S(1)}, bf16[1,4,256]{2,1,0:T(4,128)(2,1)S(1)}, u32[]{:S(2)}, u32[]{:S(2)}) collective-permute-start(bf16[1,4,256]{2,1,0:T(4,128)(2,1)S(1)} %bitcast.713), channel_id=1, source_target_pairs={{0,32},{32,64},{64,96},{96,0},{1,33},{33,65},{65,97},{97,1},{2,34}... | collective-permute-start | bytes 6152 | tf_op jit(solution)/shard_map/ppermute | solution.py:17
  22.0 3.6 %collective-permute-start = (bf16[3,4,256]{2,1,0:T(4,128)(2,1)S(1)}, bf16[3,4,256]{2,1,0:T(4,128)(2,1)S(1)}, u32[]{:S(2)}, u32[]{:S(2)}) collective-permute-start(bf16[3,4,256]{2,1,0:T(4,128)(2,1)S(1)} %pad_maximum_fusion.10), channel_id=1, source_target_pairs={{32,0},{64,32},{96,64},{0,96},{33,1},{65,33},{97,65},{1,97},{34,2}... | collective-permute-start | bytes 18440 | tf_op jit(solution)/shard_map/ppermute | solution.py:20
  24.8 3.8 %collective-permute-start.1 = (bf16[3,4,256]{2,1,0:T(4,128)(2,1)S(1)}, bf16[3,4,256]{2,1,0:T(4,128)(2,1)S(1)}, u32[]{:S(2)}, u32[]{:S(2)}) collective-permute-start(bf16[3,4,256]{2,1,0:T(4,128)(2,1)S(1)} %pad_maximum_fusion.11), channel_id=1, source_target_pairs={{0,32},{32,64},{64,96},{96,0},{1,33},{33,65},{65,97},{97,1},{2,34}... | collective-permute-start | bytes 18440 | tf_op jit(solution)/shard_map/ppermute | solution.py:17
  29.5 15.3 %all-to-all-start.1 = ((bf16[32,6,4,256]{3,2,1,0:T(4,128)(2,1)}), bf16[32,6,4,256]{3,2,1,0:T(4,128)(2,1)S(1)}, u32[]{:S(2)}, u32[]{:S(2)}) async-start(bf16[32,6,4,256]{3,2,1,0:T(4,128)(2,1)} %broadcast_in_dim.92), calls=%async_computation.1 | async-start | bytes 786432 | tf_op jit(solution)/shard_map/all_to_all | solution.py:44
  34.8 10.3 %collective-permute-start.4 = (bf16[3,1,130,256]{3,2,1,0:T(8,128)(2,1)S(1)}, bf16[3,1,130,256]{3,2,1,0:T(8,128)(2,1)S(1)}, u32[]{:S(2)}, u32[]{:S(2)}) collective-permute-start(bf16[3,1,130,256]{3,2,1,0:T(8,128)(2,1)S(1)} %get-tuple-element.166), channel_id=1, source_target_pairs={{0,1},{1,2},{2,3},{3,4},{4,5},{5,6},{6,7},{7,8},{8,9},{9,10},{10,1... | collective-permute-start | bytes 599048 | tf_op jit(solution)/shard_map/ppermute | solution.py:17
  38.4 7.2 %collective-permute-start.5 = (bf16[3,1,130,256]{3,2,1,0:T(8,128)(2,1)S(1)}, bf16[3,1,130,256]{3,2,1,0:T(8,128)(2,1)S(1)}, u32[]{:S(2)}, u32[]{:S(2)}) collective-permute-start(bf16[3,1,130,256]{3,2,1,0:T(8,128)(2,1)S(1)} %get-tuple-element.167), channel_id=1, source_target_pairs={{1,0},{2,1},{3,2},{4,3},{5,4},{6,5},{7,6},{8,7},{9,8},{10,9},{11,1... | collective-permute-start | bytes 599048 | tf_op jit(solution)/shard_map/ppermute | solution.py:20
  45.8 0.7 copy-start.8
  113.3 25.7 %copy-start.6 = (f32[7,256]{1,0:T(8,128)S(1)}, f32[7,256]{1,0:T(8,128)}, u32[]{:S(2)}) copy-start(f32[7,256]{1,0:T(8,128)} %param.18) | copy-start | bytes 21508
  129.5 24.1 %all-to-all-start.2 = ((bf16[128,3,4,1,1,256]{5,2,1,4,3,0:T(4,128)(2,1)}), bf16[128,3,4,1,1,256]{5,2,1,4,3,0:T(4,128)(2,1)S(1)}, u32[]{:S(2)}, u32[]{:S(2)}) async-start(bf16[128,3,4,1,1,256]{5,2,1,4,3,0:T(4,128)(2,1)} %constant_dynamic-update-slice_fusion.6), calls=%async_computation.2 | async-start | bytes 1572864 | tf_op jit(solution)/shard_map/all_to_all | solution.py:152
  190.0 1.5 copy-start.4
  191.5 1.1 copy-start.2
  191.8 1.2 copy-start.3
  192.9 1.2 copy-start.1
  194.6 0.7 copy-start.9
  197.9 21.1 %all-to-all-start.3 = ((bf16[3,4,1,128,256]{4,1,2,0,3:T(4,128)(2,1)}), bf16[3,4,1,128,256]{4,1,2,0,3:T(4,128)(2,1)S(1)}, u32[]{:S(2)}, u32[]{:S(2)}) async-start(bf16[3,4,1,128,256]{4,1,2,0,3:T(4,128)(2,1)} %copy.445), calls=%async_computation.3 | async-start | bytes 1572864 | tf_op jit(solution)/shard_map/all_to_all | solution.py:182
  222.2 0.7 copy-start.5
  222.2 0.7 copy-start.12
  222.9 1.0 copy-start.10
  222.9 1.1 copy-start.11
  228.6 1.0 copy-start.10
  228.6 1.1 copy-start.11
  234.3 1.0 copy-start.10
  234.3 1.1 copy-start.11
